TPU v7x, 256 devices: a whole 4x4x8 slice. The times are simulated.
256 devices in a mesh: pipe: 8 (over y, core), expert: 32 (over x, z).
Axes of the slice: x: 4, y: 4, z: 8, core: 2. Of those that a mesh axis runs over, the one named last changes fastest.
Arguments:
- state: bfloat16 [8, 1536, 2048], P('pipe', 'expert'), may hold values from -6 to 6
- route_ids: int32 [3, 8, 1536, 8], P(None, 'pipe', 'expert'), may hold values from 0 to 31, all different within a row; in each aligned block of 48 rows (0 to 47, 48 to 95, ..., all dimensions but the last counted through in order) at most 16 rows name the same one
- route_weights: float32 [3, 8, 1536, 8], P(None, 'pipe', 'expert'), may hold values from 0.02 to 0.3
- norm_gain: float32 [8, 2048], P('pipe'), may hold values from 0.1 to 1.9
- w_gate: bfloat16 [8, 32, 2048, 768], P('pipe', 'expert'), may hold values from -0.125 to 0.125
- w_up: bfloat16 [8, 32, 2048, 768], P('pipe', 'expert'), may hold values from -0.125 to 0.125
- w_down: bfloat16 [8, 32, 768, 2048], P('pipe', 'expert'), may hold values from -0.21875 to 0.21875
Outputs:
- final_state: bfloat16 [8, 1536, 2048], P('pipe', 'expert')
Inputs may be any that keep to these rules, and one draw needn't show every extreme that they name: `route_ids`: each token names 8 different experts. In the routes of one device (a block of 48 tokens of one step and section) no expert is named more than 16 times, and in every draw some block names an expert exactly 16 times.
All inputs are finite; a program needn't handle non-finite values.
Results may differ from a plain program's by a relative error of at most 0.0065.
Values may be sent and summed in bfloat16 or wider, within the bound.
No kernel may reach another device: no remote copies, remote signals or barrier semaphores. Data moves between devices by JAX's collectives and lax.ppermute only.
A program may use at most 64 MiB of HBM per device.

v0:
```python
import jax
import jax.numpy as jnp
from jax import lax
from jax.sharding import PartitionSpec as P


def shifted(array, axis, by):
    size = lax.axis_size(axis)
    return lax.ppermute(array, axis, [(i, (i + by) % size) for i in range(size)])


def expert_ffn(rows, gate_weight, up_weight, down_weight):
    shape = rows.shape
    flat = rows.reshape(-1, shape[-1])
    gate = jnp.dot(flat, gate_weight, preferred_element_type=jnp.float32)
    upper = jnp.dot(flat, up_weight, preferred_element_type=jnp.float32)
    hidden = (jax.nn.silu(gate) * upper).astype(jnp.bfloat16)
    output = jnp.dot(hidden, down_weight, preferred_element_type=jnp.float32).astype(jnp.bfloat16)
    return output.reshape(shape[:-1] + (down_weight.shape[1],))


def shards(state, route_ids, route_weights, norm_gain, w_gate, w_up, w_down):
    experts = lax.axis_size("expert")
    owner = lax.axis_index("expert")
    panel_rows = state.shape[1]
    width = state.shape[2]
    chosen = route_ids.shape[3]
    capacity = min(panel_rows, 4 * panel_rows * chosen // (3 * experts))
    gain = norm_gain[0]
    gate_weight = w_gate[0, 0]
    up_weight = w_up[0, 0]
    down_weight = w_down[0, 0]
    panel = state[0]
    for tick_index in range(route_ids.shape[0]):
        section_ids = route_ids[tick_index, 0]
        section_wts = route_weights[tick_index, 0]
        widened = panel.astype(jnp.float32)
        scale = lax.rsqrt(jnp.mean(widened * widened, axis=-1, keepdims=True) + 1e-06)
        normed = (widened * scale * gain).astype(jnp.bfloat16)
        matches = (section_ids.reshape(-1)[:, None] == jnp.arange(experts, dtype=jnp.int32)).astype(
            jnp.int32
        )
        ranks = jnp.cumsum(matches, axis=0) - 1
        slot_of = jnp.sum(ranks * matches, axis=1)
        position = section_ids.reshape(-1) * capacity + slot_of
        all_rows, all_ids = (
            lax.all_gather(normed, "expert", axis=0, tiled=True),
            lax.all_gather(section_ids, "expert", axis=0, tiled=True),
        )
        hit_token = jnp.sum((all_ids == owner).astype(jnp.int32), axis=1)
        hit_blocks = hit_token.reshape(experts, panel_rows)
        block_rank = jnp.cumsum(hit_blocks, axis=1) - 1
        sources = jnp.arange(experts, dtype=jnp.int32)[:, None]
        target = jnp.where(
            hit_blocks > 0, sources * capacity + block_rank, experts * capacity
        ).reshape(-1)
        every_token = jnp.arange(experts * panel_rows, dtype=jnp.int32)
        slot_token = (
            jnp.zeros((experts * capacity,), jnp.int32).at[target].set(every_token, mode="drop")
        )
        filled = jnp.zeros((experts * capacity,), jnp.int32).at[target].set(1, mode="drop")
        incoming = jnp.where(filled[:, None] > 0, all_rows[slot_token], jnp.zeros((), jnp.bfloat16))
        results = expert_ffn(
            incoming.reshape(experts, capacity, width), gate_weight, up_weight, down_weight
        )
        returned = lax.all_to_all(results, "expert", split_axis=0, concat_axis=0, tiled=True)
        picked = returned.reshape(experts * capacity, width)[position].reshape(
            panel_rows, chosen, width
        )
        combined = jnp.sum(section_wts[:, :, None] * picked.astype(jnp.float32), axis=1)
        updated = (widened + combined).astype(jnp.bfloat16)
        panel = shifted(updated, "pipe", 1)
    return panel[None]


def solution(mesh):
    placed = (
        P("pipe", "expert", None),
        P(None, "pipe", "expert", None),
        P(None, "pipe", "expert", None),
        P("pipe", None),
        P("pipe", "expert", None, None),
        P("pipe", "expert", None, None),
        P("pipe", "expert", None, None),
    )
    return jax.shard_map(
        shards, mesh=mesh, in_specs=placed, out_specs=P("pipe", "expert", None), check_vma=False
    )
```

profile of v0, /device:TPU:32, one launch (start us, length us, event | category | flops | bytes accessed | tf_op | source)
XLA Modules:
  0.0 707.4 jit_solution(3878133319197394416)
XLA Ops:
  10.5 52.2 %all-gather.1 = s32[1,1,1536,8]{3,1,0,2:T(1,128)S(1)} all-gather(s32[1,1,48,8]{3,1,0,2:T(1,128)S(1)} %copy.36), channel_id=3, replica_groups=mesh['pipe'=8,'expert'=32] {'expert'}, dimensions={2}, use_global_device_ids=true | all-gather | bytes 50688 | tf_op jit(solution)/shard_map/all_gather | solution.py:48
  62.7 49.0 %all-gather = s32[1,1,1536,8]{3,1,0,2:T(1,128)S(1)} all-gather(s32[1,1,48,8]{3,1,0,2:T(1,128)S(1)} %copy.35), channel_id=2, replica_groups=mesh['pipe'=8,'expert'=32] {'expert'}, dimensions={2}, use_global_device_ids=true | all-gather | bytes 50688 | tf_op jit(solution)/shard_map/all_gather | solution.py:48
  111.7 63.2 %fusion.42 = (s32[1536]{0:T(1024)S(1)}, s32[1536]{0:T(1024)S(1)}) fusion(s32[1,1,1536,8]{3,1,0,2:T(1,128)S(1)} %all-gather, s32[]{:T(128)S(6)} %axis_index.12, s32[1,1,1536,8]{3,1,0,2:T(1,128)S(1)} %all-gather.1), kind=kLoop, calls=%fused_computation.48 | loop fusion | flops 70656 | bytes 110596 | tf_op jit(solution)/shard_map/reduce_sum | solution.py:50
  175.4 48.6 %all-gather.2 = s32[1,1,1536,8]{3,1,0,2:T(1,128)S(1)} all-gather(s32[1,1,48,8]{3,1,0,2:T(1,128)S(1)} %copy.37), channel_id=4, replica_groups=mesh['pipe'=8,'expert'=32] {'expert'}, dimensions={2}, use_global_device_ids=true | all-gather | bytes 50688 | tf_op jit(solution)/shard_map/all_gather | solution.py:48
  224.0 27.3 %fusion.44 = s32[1536]{0:T(1024)S(1)} fusion(s32[1,1,1536,8]{3,1,0,2:T(1,128)S(1)} %all-gather.2, s32[]{:T(128)S(6)} %axis_index.12), kind=kLoop, calls=%fused_computation.50 | loop fusion | flops 35328 | bytes 55300 | tf_op jit(solution)/shard_map/reduce_sum | solution.py:50
  251.8 6.2 scatter_custom_fusion.1
  258.0 6.4 scatter_custom_fusion
  264.4 8.8 %gather_fusion = bf16[512,2048]{1,0:T(8,128)(2,1)} fusion(bf16[1536,2048]{1,0:T(8,128)(2,1)} %all-gather.7.cloned.1.call-done, s32[1024]{0:T(1024)S(1)} %pad_clamp_fusion.5), kind=kCustom, calls=%fused_computation | custom fusion | bytes 4196352 | tf_op jit(solution)/shard_map/gather | solution.py:62
  278.8 8.3 %fusion.21 = bf16[512,2048]{1,0:T(8,128)(2,1)} fusion(bf16[1,1,768,2048]{3,2,1,0:T(8,128)(2,1)S(1)} %copy-done, f32[512,768]{1,0:T(8,128)} %fusion.19, bf16[1,1,2048,768]{3,2,1,0:T(8,128)(2,1)} %param.12, bf16[512,2048]{1,0:T(8,128)(2,1)} %gather_fusion, pred[512]{0:T(512)(128)(4,1)S(1)} %broadcast_compare_fusion.5), kind=kOutput, calls=%fused_computation.39 | convolution fusion | flops 3225681920 | bytes 12059136 | tf_op jit(solution)/shard_map/dot_general | solution.py:18
  287.1 7.3 %all-to-all-start = ((bf16[32,16,2048]{2,1,0:T(8,128)(2,1)}), bf16[32,16,2048]{2,1,0:T(8,128)(2,1)}, u32[]{:S(2)}, u32[]{:S(2)}) async-start(bf16[32,16,2048]{2,1,0:T(8,128)(2,1)} %bitcast.127), calls=%async_computation | async-start | bytes 4194304 | tf_op jit(solution)/shard_map/all_to_all | solution.py:66
  296.6 27.9 %all-to-all-done = bf16[32,16,2048]{2,1,0:T(8,128)(2,1)} async-done(((bf16[32,16,2048]{2,1,0:T(8,128)(2,1)}), bf16[32,16,2048]{2,1,0:T(8,128)(2,1)}, u32[]{:S(2)}, u32[]{:S(2)}) %all-to-all-start) | async-done | bytes 2097184 | tf_op jit(solution)/shard_map/all_to_all | solution.py:66
  324.5 6.9 gather_fusion.1
  334.4 6.3 collective-permute-done
  341.8 6.2 scatter_custom_fusion.2
  348.0 6.2 scatter_custom_fusion.3
  354.2 71.4 %all-gather.9.cloned.1.call-done = bf16[1536,2048]{1,0:T(8,128)(2,1)} async-done(((bf16[48,2048]{1,0:T(8,128)(2,1)}), bf16[1536,2048]{1,0:T(8,128)(2,1)}) %all-gather.9.cloned.1.call-update) | async-done | bytes 6291472 | tf_op jit(solution)/shard_map/all_gather | solution.py:47
  425.6 9.3 %gather_fusion.2 = bf16[512,2048]{1,0:T(8,128)(2,1)} fusion(bf16[1536,2048]{1,0:T(8,128)(2,1)} %all-gather.9.cloned.1.call-done, s32[1024]{0:T(1024)S(1)} %pad_clamp_fusion.3), kind=kCustom, calls=%fused_computation.2 | custom fusion | bytes 4196352 | tf_op jit(solution)/shard_map/gather | solution.py:62
  434.9 5.5 fusion.17
  440.4 8.3 %fusion.24 = bf16[512,2048]{1,0:T(8,128)(2,1)} fusion(bf16[1,1,768,2048]{3,2,1,0:T(8,128)(2,1)S(1)} %copy-done, f32[512,768]{1,0:T(8,128)} %fusion.17, bf16[1,1,2048,768]{3,2,1,0:T(8,128)(2,1)} %param.12, bf16[512,2048]{1,0:T(8,128)(2,1)} %gather_fusion.2, pred[512]{0:T(512)(128)(4,1)S(1)} %broadcast_compare_fusion.4), kind=kOutput, calls=%fused_computation.40 | convolution fusion | flops 3225681920 | bytes 12059136 | tf_op jit(solution)/shard_map/dot_general | solution.py:18
  448.8 5.8 all-to-all-start.1
  456.6 47.4 %all-to-all-done.1 = bf16[32,16,2048]{2,1,0:T(8,128)(2,1)} async-done(((bf16[32,16,2048]{2,1,0:T(8,128)(2,1)}), bf16[32,16,2048]{2,1,0:T(8,128)(2,1)}, u32[]{:S(2)}, u32[]{:S(2)}) %all-to-all-start.1) | async-done | bytes 2097184 | tf_op jit(solution)/shard_map/all_to_all | solution.py:66
  504.0 6.9 gather_fusion.3
  513.9 6.3 collective-permute-done.1
  521.3 6.2 scatter_custom_fusion.4
  527.5 6.2 scatter_custom_fusion.5
  533.7 72.1 %all-gather.11.cloned.1.call-done = bf16[1536,2048]{1,0:T(8,128)(2,1)} async-done(((bf16[48,2048]{1,0:T(8,128)(2,1)}), bf16[1536,2048]{1,0:T(8,128)(2,1)}) %all-gather.11.cloned.1.call-update) | async-done | bytes 6291472 | tf_op jit(solution)/shard_map/all_gather | solution.py:47
  605.8 9.0 %gather_fusion.4 = bf16[512,2048]{1,0:T(8,128)(2,1)} fusion(bf16[1536,2048]{1,0:T(8,128)(2,1)} %all-gather.11.cloned.1.call-done, s32[1024]{0:T(1024)S(1)} %pad_clamp_fusion.1), kind=kCustom, calls=%fused_computation.4 | custom fusion | bytes 4196352 | tf_op jit(solution)/shard_map/gather | solution.py:62
  620.4 8.3 %fusion.27 = bf16[512,2048]{1,0:T(8,128)(2,1)} fusion(bf16[1,1,768,2048]{3,2,1,0:T(8,128)(2,1)S(1)} %copy-done, f32[512,768]{1,0:T(8,128)} %fusion.15, bf16[1,1,2048,768]{3,2,1,0:T(8,128)(2,1)} %param.12, bf16[512,2048]{1,0:T(8,128)(2,1)} %gather_fusion.4, pred[512]{0:T(512)(128)(4,1)S(1)} %broadcast_compare_fusion.3), kind=kOutput, calls=%fused_computation.41 | convolution fusion | flops 3225681920 | bytes 12059136 | tf_op jit(solution)/shard_map/dot_general | solution.py:18
  628.7 5.8 all-to-all-start.2
  636.4 47.3 %all-to-all-done.2 = bf16[32,16,2048]{2,1,0:T(8,128)(2,1)} async-done(((bf16[32,16,2048]{2,1,0:T(8,128)(2,1)}), bf16[32,16,2048]{2,1,0:T(8,128)(2,1)}, u32[]{:S(2)}, u32[]{:S(2)}) %all-to-all-start.2) | async-done | bytes 2097184 | tf_op jit(solution)/shard_map/all_to_all | solution.py:66
  683.7 6.9 gather_fusion.5
  693.6 6.3 collective-permute-done.2
  (110 shorter events, 33.6 us)
Async XLA Ops:
  6.5 272.2 %copy-start = (bf16[1,1,768,2048]{3,2,1,0:T(8,128)(2,1)S(1)}, bf16[1,1,768,2048]{3,2,1,0:T(8,128)(2,1)}, u32[]{:S(2)}) copy-start(bf16[1,1,768,2048]{3,2,1,0:T(8,128)(2,1)} %param.13) | copy-start | bytes 9437188
  6.5 257.9 %all-gather.7.cloned.1.call-start = ((), (), s32[]{:S(2)}) async-start(), calls=%async_computation.3 | async-start | bytes 6488064 | tf_op jit(solution)/shard_map/all_gather | solution.py:47
  287.1 7.6 %copy-start.3 = (f32[3,1,48,8]{2,3,1,0:T(8,128)S(1)}, f32[3,1,48,8]{2,3,1,0:T(8,128)}, u32[]{:S(2)}) copy-start(f32[3,1,48,8]{2,3,1,0:T(8,128)} %param.9) | copy-start | bytes 13828
  287.1 37.4 %all-to-all-start = ((bf16[32,16,2048]{2,1,0:T(8,128)(2,1)}), bf16[32,16,2048]{2,1,0:T(8,128)(2,1)}, u32[]{:S(2)}, u32[]{:S(2)}) async-start(bf16[32,16,2048]{2,1,0:T(8,128)(2,1)} %bitcast.127), calls=%async_computation | async-start | bytes 4194304 | tf_op jit(solution)/shard_map/all_to_all | solution.py:66
  294.4 131.2 %all-gather.9.cloned.1.call-start = ((), (), s32[]{:S(2)}) async-start(), calls=%async_computation.4 | async-start | bytes 6488064 | tf_op jit(solution)/shard_map/all_gather | solution.py:47
  331.4 2.9 copy-start.1
  331.4 9.4 %copy-start.2 = (f32[1,2048]{1,0:T(1,128)S(1)}, f32[1,2048]{1,0:T(1,128)}, u32[]{:S(2)}) copy-start(f32[1,2048]{1,0:T(1,128)} %param.10) | copy-start | bytes 24580
  334.4 6.3 collective-permute-start
  448.8 55.2 %all-to-all-start.1 = ((bf16[32,16,2048]{2,1,0:T(8,128)(2,1)}), bf16[32,16,2048]{2,1,0:T(8,128)(2,1)}, u32[]{:S(2)}, u32[]{:S(2)}) async-start(bf16[32,16,2048]{2,1,0:T(8,128)(2,1)} %bitcast.129), calls=%async_computation.1 | async-start | bytes 4194304 | tf_op jit(solution)/shard_map/all_to_all | solution.py:66
  454.6 151.2 %all-gather.11.cloned.1.call-start = ((), (), s32[]{:S(2)}) async-start(), calls=%async_computation.5 | async-start | bytes 6488064 | tf_op jit(solution)/shard_map/all_gather | solution.py:47
  513.9 6.3 collective-permute-start.1
  628.7 55.0 %all-to-all-start.2 = ((bf16[32,16,2048]{2,1,0:T(8,128)(2,1)}), bf16[32,16,2048]{2,1,0:T(8,128)(2,1)}, u32[]{:S(2)}, u32[]{:S(2)}) async-start(bf16[32,16,2048]{2,1,0:T(8,128)(2,1)} %bitcast.128), calls=%async_computation.2 | async-start | bytes 4194304 | tf_op jit(solution)/shard_map/all_to_all | solution.py:66
  693.6 6.3 collective-permute-start.2
Sparse Core Ops, SparseCore 0:
  9.9 92.9 all-gather.6
  341.8 83.7 all-gather.8
  521.3 84.5 all-gather.10
where the time goes:
time: 708 us; the launch traced here: 707 us
  waiting for transfers between devices  285 us (40%)
  blocking collectives  150 us (21%)
  other arithmetic  109 us (15%)
  local copies, waits for them, and re-layouts  89.3 us (13%)
  matrix products  41.6 us (6%)
  starting transfers between devices  19.1 us (3%)
  between operations  13.9 us (2%)
    all_gather x3, blocking collectives, shards(): lax.all_gather(section_ids, 'expert', axis=0, tiled=True)  150 us
    all_gather x3, waiting for transfers between devices, shards(): lax.all_gather(normed, 'expert', axis=0, tiled=True)  144 us
    all_to_all x3, waiting for transfers between devices, shards(): lax.all_to_all(results, 'expert', split_axis=0, concat_axis=0, tiled=True)  123 us
    reduce_sum x2, other arithmetic, shards(): hit_token = jnp.sum((all_ids == owner).astype(jnp.int32), axis=1)  90.4 us
    gather x3, local copies, waits for them, and re-layouts, shards(): all_rows[slot_token]  27.1 us
    dot_general x3, matrix products, expert_ffn(): jnp.dot(hidden, down_weight, preferred_element_type=jnp.float32)  25 us
    gather x3, local copies, waits for them, and re-layouts, shards(): returned.reshape(experts * capacity, width)[position]  20.8 us
    all_to_all x3, starting transfers between devices, shards(): lax.all_to_all(results, 'expert', split_axis=0, concat_axis=0, tiled=True)  19 us
  transfers between devices with their start and end apart: 9, of which 8 were waited for; matrix products, arithmetic and copies ran while one was open for 19% of the time, Pallas kernels for 0%

commit v1 on v0

--- a/solution.py
+++ b/solution.py
@@ -44,7 +44,10 @@
         slot_of = jnp.sum(ranks * matches, axis=1)
         position = section_ids.reshape(-1) * capacity + slot_of
         all_rows, all_ids = (
-            lax.all_gather(normed, "expert", axis=0, tiled=True),
+            jnp.concatenate(
+                lax.all_to_all(jnp.stack([normed] * lax.axis_size("expert")), "expert", 0, 0),
+                axis=0,
+            ),
             lax.all_gather(section_ids, "expert", axis=0, tiled=True),
         )
         hit_token = jnp.sum((all_ids == owner).astype(jnp.int32), axis=1)

time: 708 us -> 978 us (1.38)
  blocking collectives: 150 us -> 278 us
  waiting for transfers between devices: 285 us -> 394 us
  starting transfers between devices: 19.1 us -> 48.6 us
  between operations: 13.9 us -> 0.75 us
    all_to_all x0 -> x3, waiting for transfers between devices: none -> 253 us  [shards(): lax.all_to_all(jnp.stack([normed] * lax.axis_size('expert')), 'expert', 0...]
    all_gather x3 -> x0, waiting for transfers between devices: 144 us -> none  [shards(): lax.all_gather(normed, 'expert', axis=0, tiled=True)]
    all_gather x3, blocking collectives: 150 us -> 278 us  [shards(): lax.all_gather(section_ids, 'expert', axis=0, tiled=True)]
    all_to_all x0 -> x3, starting transfers between devices: none -> 23.9 us  [shards(): lax.all_to_all(jnp.stack([normed] * lax.axis_size('expert')), 'expert', 0...]
    another operation x3 -> x6, local copies, waits for them, and re-layouts: 0.44 us -> 10.8 us  [the longest x3 10.4 us: shards(): jnp.stack([normed] * lax.axis_size('expert'))]
  transfers between devices with their start and end apart: 9 -> 9, of which waited for: 8 -> 8; matrix products, arithmetic and copies ran while one was open for 19% -> 14% of each run, Pallas kernels for 0% -> 0%
where the time goes in v1:
time: 978 us; the launch traced here: 973 us
  waiting for transfers between devices  394 us (40%)
  blocking collectives  278 us (28%)
  other arithmetic  112 us (11%)
  local copies, waits for them, and re-layouts  98.6 us (10%)
  starting transfers between devices  48.6 us (5%)
  matrix products  41.6 us (4%)
    all_gather x3, blocking collectives, shards(): lax.all_gather(section_ids, 'expert', axis=0, tiled=True)  278 us
    all_to_all x3, waiting for transfers between devices, shards(): lax.all_to_all(jnp.stack([normed] * lax.axis_size('expert')), 'expert', 0...  253 us
    all_to_all x3, waiting for transfers between devices, shards(): lax.all_to_all(results, 'expert', split_axis=0, concat_axis=0, tiled=True)  122 us
    reduce_sum x2, other arithmetic, shards(): hit_token = jnp.sum((all_ids == owner).astype(jnp.int32), axis=1)  96.4 us
    gather x3, local copies, waits for them, and re-layouts, shards(): all_rows[slot_token]  26.9 us
    dot_general x3, matrix products, expert_ffn(): jnp.dot(hidden, down_weight, preferred_element_type=jnp.float32)  25 us
    all_to_all x3, starting transfers between devices, shards(): lax.all_to_all(results, 'expert', split_axis=0, concat_axis=0, tiled=True)  24.6 us
    all_to_all x3, starting transfers between devices, shards(): lax.all_to_all(jnp.stack([normed] * lax.axis_size('expert')), 'expert', 0...  23.9 us
  transfers between devices with their start and end apart: 9, of which 8 were waited for; matrix products, arithmetic and copies ran while one was open for 14% of the time, Pallas kernels for 0%

profile of v1, /device:TPU:32, one launch (start us, length us, event | category | flops | bytes accessed | tf_op | source)
XLA Modules:
  0.0 973.4 jit_solution(12512370641007549305)
XLA Ops:
  5.7 11.4 %all-to-all-start = ((bf16[32,48,2048]{2,1,0:T(8,128)(2,1)}), bf16[32,48,2048]{2,1,0:T(8,128)(2,1)}, u32[]{:S(2)}, u32[]{:S(2)}) async-start(bf16[32,48,2048]{2,1,0:T(8,128)(2,1)} %stack.9), calls=%async_computation | async-start | bytes 12582912 | tf_op jit(solution)/shard_map/all_to_all | solution.py:48
  17.4 181.7 %all-gather.1 = s32[1,1,1536,8]{3,1,0,2:T(1,128)S(1)} all-gather(s32[1,1,48,8]{3,1,0,2:T(1,128)S(1)} %copy.36), channel_id=3, replica_groups=mesh['pipe'=8,'expert'=32] {'expert'}, dimensions={2}, use_global_device_ids=true | all-gather | bytes 50688 | tf_op jit(solution)/shard_map/all_gather | solution.py:51
  199.0 47.6 %all-gather = s32[1,1,1536,8]{3,1,0,2:T(1,128)S(1)} all-gather(s32[1,1,48,8]{3,1,0,2:T(1,128)S(1)} %copy.35), channel_id=2, replica_groups=mesh['pipe'=8,'expert'=32] {'expert'}, dimensions={2}, use_global_device_ids=true | all-gather | bytes 50688 | tf_op jit(solution)/shard_map/all_gather | solution.py:51
  246.6 69.1 %fusion.42 = (s32[1536]{0:T(1024)S(1)}, s32[1536]{0:T(1024)S(1)}) fusion(s32[1,1,1536,8]{3,1,0,2:T(1,128)S(1)} %all-gather, s32[]{:T(128)S(6)} %axis_index.12, s32[1,1,1536,8]{3,1,0,2:T(1,128)S(1)} %all-gather.1), kind=kLoop, calls=%fused_computation.48 | loop fusion | flops 70656 | bytes 110596 | tf_op jit(solution)/shard_map/reduce_sum | solution.py:53
  316.3 48.6 %all-gather.2 = s32[1,1,1536,8]{3,1,0,2:T(1,128)S(1)} all-gather(s32[1,1,48,8]{3,1,0,2:T(1,128)S(1)} %copy.37), channel_id=4, replica_groups=mesh['pipe'=8,'expert'=32] {'expert'}, dimensions={2}, use_global_device_ids=true | all-gather | bytes 50688 | tf_op jit(solution)/shard_map/all_gather | solution.py:51
  364.9 27.3 %fusion.44 = s32[1536]{0:T(1024)S(1)} fusion(s32[1,1,1536,8]{3,1,0,2:T(1,128)S(1)} %all-gather.2, s32[]{:T(128)S(6)} %axis_index.12), kind=kLoop, calls=%fused_computation.50 | loop fusion | flops 35328 | bytes 55300 | tf_op jit(solution)/shard_map/reduce_sum | solution.py:53
  392.7 6.2 scatter_custom_fusion.1
  398.9 6.3 scatter_custom_fusion
  405.3 8.8 gather_fusion
  419.6 8.3 fusion.21
  427.9 8.3 all-to-all-start.1
  438.0 28.0 %all-to-all-done.1 = bf16[32,16,2048]{2,1,0:T(8,128)(2,1)} async-done(((bf16[32,16,2048]{2,1,0:T(8,128)(2,1)}), bf16[32,16,2048]{2,1,0:T(8,128)(2,1)}, u32[]{:S(2)}, u32[]{:S(2)}) %all-to-all-start.1) | async-done | bytes 2097184 | tf_op jit(solution)/shard_map/all_to_all | solution.py:69
  466.0 6.9 gather_fusion.1
  476.0 6.3 collective-permute-done
  491.4 6.2 scatter_custom_fusion.2
  497.6 6.2 scatter_custom_fusion.3
  503.8 125.8 %all-to-all-done.2 = bf16[32,48,2048]{2,1,0:T(8,128)(2,1)} async-done(((bf16[32,48,2048]{2,1,0:T(8,128)(2,1)}), bf16[32,48,2048]{2,1,0:T(8,128)(2,1)}, u32[]{:S(2)}, u32[]{:S(2)}) %all-to-all-start.2) | async-done | bytes 6291488 | tf_op jit(solution)/shard_map/all_to_all | solution.py:48
  629.6 9.2 gather_fusion.2
  644.3 8.3 fusion.24
  652.7 7.7 all-to-all-start.3
  662.2 47.2 %all-to-all-done.3 = bf16[32,16,2048]{2,1,0:T(8,128)(2,1)} async-done(((bf16[32,16,2048]{2,1,0:T(8,128)(2,1)}), bf16[32,16,2048]{2,1,0:T(8,128)(2,1)}, u32[]{:S(2)}, u32[]{:S(2)}) %all-to-all-start.3) | async-done | bytes 2097184 | tf_op jit(solution)/shard_map/all_to_all | solution.py:69
  709.4 6.9 gather_fusion.3
  719.3 6.3 collective-permute-done.1
  729.3 7.3 all-to-all-start.4
  742.9 6.2 scatter_custom_fusion.5
  749.1 126.8 %all-to-all-done.4 = bf16[32,48,2048]{2,1,0:T(8,128)(2,1)} async-done(((bf16[32,48,2048]{2,1,0:T(8,128)(2,1)}), bf16[32,48,2048]{2,1,0:T(8,128)(2,1)}, u32[]{:S(2)}, u32[]{:S(2)}) %all-to-all-start.4) | async-done | bytes 6291488 | tf_op jit(solution)/shard_map/all_to_all | solution.py:48
  875.9 8.8 gather_fusion.4
  890.2 8.3 fusion.27
  898.6 8.7 all-to-all-start.5
  909.1 47.2 %all-to-all-done.5 = bf16[32,16,2048]{2,1,0:T(8,128)(2,1)} async-done(((bf16[32,16,2048]{2,1,0:T(8,128)(2,1)}), bf16[32,16,2048]{2,1,0:T(8,128)(2,1)}, u32[]{:S(2)}, u32[]{:S(2)}) %all-to-all-start.5) | async-done | bytes 2097184 | tf_op jit(solution)/shard_map/all_to_all | solution.py:69
  956.3 6.9 gather_fusion.5
  966.2 6.3 collective-permute-done.2
  (112 shorter events, 57.6 us)
Async XLA Ops:
  0.0 419.6 %copy-start = (bf16[1,1,768,2048]{3,2,1,0:T(8,128)(2,1)S(1)}, bf16[1,1,768,2048]{3,2,1,0:T(8,128)(2,1)}, u32[]{:S(2)}) copy-start(bf16[1,1,768,2048]{3,2,1,0:T(8,128)(2,1)} %param.13) | copy-start | bytes 9437188
  5.7 11.4 %copy-start.4 = (s32[3,1,48,8]{2,3,1,0:T(8,128)S(1)}, s32[3,1,48,8]{2,3,1,0:T(8,128)}, u32[]{:S(2)}) copy-start(s32[3,1,48,8]{2,3,1,0:T(8,128)} %param.8) | copy-start | bytes 13828
  5.7 399.5 %all-to-all-start = ((bf16[32,48,2048]{2,1,0:T(8,128)(2,1)}), bf16[32,48,2048]{2,1,0:T(8,128)(2,1)}, u32[]{:S(2)}, u32[]{:S(2)}) async-start(bf16[32,48,2048]{2,1,0:T(8,128)(2,1)} %stack.9), calls=%async_computation | async-start | bytes 12582912 | tf_op jit(solution)/shard_map/all_to_all | solution.py:48
  427.9 8.5 copy-start.3
  427.9 38.1 %all-to-all-start.1 = ((bf16[32,16,2048]{2,1,0:T(8,128)(2,1)}), bf16[32,16,2048]{2,1,0:T(8,128)(2,1)}, u32[]{:S(2)}, u32[]{:S(2)}) async-start(bf16[32,16,2048]{2,1,0:T(8,128)(2,1)} %bitcast.137), calls=%async_computation.1 | async-start | bytes 4194304 | tf_op jit(solution)/shard_map/all_to_all | solution.py:69
  473.0 2.9 copy-start.1
  473.0 9.4 copy-start.2
  476.0 6.3 collective-permute-start
  486.0 143.6 %all-to-all-start.2 = ((bf16[32,48,2048]{2,1,0:T(8,128)(2,1)}), bf16[32,48,2048]{2,1,0:T(8,128)(2,1)}, u32[]{:S(2)}, u32[]{:S(2)}) async-start(bf16[32,48,2048]{2,1,0:T(8,128)(2,1)} %stack.10), calls=%async_computation.2 | async-start | bytes 12582912 | tf_op jit(solution)/shard_map/all_to_all | solution.py:48
  652.7 56.7 %all-to-all-start.3 = ((bf16[32,16,2048]{2,1,0:T(8,128)(2,1)}), bf16[32,16,2048]{2,1,0:T(8,128)(2,1)}, u32[]{:S(2)}, u32[]{:S(2)}) async-start(bf16[32,16,2048]{2,1,0:T(8,128)(2,1)} %bitcast.139), calls=%async_computation.3 | async-start | bytes 4194304 | tf_op jit(solution)/shard_map/all_to_all | solution.py:69
  719.2 6.3 collective-permute-start.1
  729.3 146.6 %all-to-all-start.4 = ((bf16[32,48,2048]{2,1,0:T(8,128)(2,1)}), bf16[32,48,2048]{2,1,0:T(8,128)(2,1)}, u32[]{:S(2)}, u32[]{:S(2)}) async-start(bf16[32,48,2048]{2,1,0:T(8,128)(2,1)} %stack.11), calls=%async_computation.4 | async-start | bytes 12582912 | tf_op jit(solution)/shard_map/all_to_all | solution.py:48
  898.6 57.8 %all-to-all-start.5 = ((bf16[32,16,2048]{2,1,0:T(8,128)(2,1)}), bf16[32,16,2048]{2,1,0:T(8,128)(2,1)}, u32[]{:S(2)}, u32[]{:S(2)}) async-start(bf16[32,16,2048]{2,1,0:T(8,128)(2,1)} %bitcast.138), calls=%async_computation.5 | async-start | bytes 4194304 | tf_op jit(solution)/shard_map/all_to_all | solution.py:69
  966.2 6.3 collective-permute-start.2
